TPU v7x, 32 devices: a whole 2x2x4 slice. The times are simulated.
32 devices in a mesh: section: 2 (over y), tensor: 4 (over z), fsdp: 4 (over x, core).
Axes of the slice: x: 2, y: 2, z: 4, core: 2. Of those that a mesh axis runs over, the one named last changes fastest.
Arguments:
- images: bfloat16 [2, 4, 729, 1152], P(None, 'fsdp'), may hold values from -6 to 6
- cotangent: bfloat16 [2, 4, 729, 1152], P(None, 'fsdp'), may hold values from -6 to 6
- qkv_weight: bfloat16 [2, 3, 1152, 1152], P('section', None, 'fsdp', 'tensor'), may hold values from -1 to 1
- qv_bias: bfloat16 [2, 2, 1152], P('section', None, 'tensor'), may hold values from -3 to 3
- out_weight: bfloat16 [2, 1152, 1152], P('section', 'tensor', 'fsdp'), may hold values from -0.75 to 0.75
- up_weight: bfloat16 [2, 1152, 4304], P('section', 'fsdp', 'tensor'), may hold values from -0.1875 to 0.1875
- up_bias: bfloat16 [2, 4304], P('section', 'tensor'), may hold values from -3 to 3
- down_weight: bfloat16 [2, 4304, 1152], P('section', 'tensor', 'fsdp'), may hold values from -0.09375 to 0.09375
- gains: bfloat16 [2, 2, 1152], P('section', None, 'fsdp'), may hold values from 0.099609375 to 1.8984375
- shifts: bfloat16 [2, 4, 1152], P('section', None, 'fsdp'), may hold values from -3 to 3
Outputs:
- section_outputs: bfloat16 [2, 2, 4, 729, 1152], P('section', None, 'fsdp')
- input_grads: bfloat16 [2, 2, 4, 729, 1152], P('section', None, 'fsdp')
- grad_qkv: float32 [2, 3, 1152, 1152], P('section', None, 'fsdp', 'tensor')
- grad_qv_bias: float32 [2, 2, 1152], P('section', None, 'tensor')
- grad_out: float32 [2, 1152, 1152], P('section', 'tensor', 'fsdp')
- grad_up: float32 [2, 1152, 4304], P('section', 'fsdp', 'tensor')
- grad_up_bias: float32 [2, 4304], P('section', 'tensor')
- grad_down: float32 [2, 4304, 1152], P('section', 'tensor', 'fsdp')
- grad_gains: float32 [2, 2, 1152], P('section', None, 'fsdp')
- grad_shifts: float32 [2, 4, 1152], P('section', None, 'fsdp')
All inputs are finite; a program needn't handle non-finite values.
Results may differ from a plain program's by a relative error of at most 0.013.
Values may be sent and summed in bfloat16 or wider, within the bound.
A program may use at most 256 MiB of HBM per device.

v0:
```python
import jax
import jax.numpy as jnp
from jax import lax
from jax.sharding import PartitionSpec as P

HD = 72
NORM_EPS = 1e-06
GELU_ROOT = 0.7978845608028654
GELU_CUBIC = 0.044715


def from_behind(value, axis, steps):
    count = lax.axis_size(axis)
    leading, last = (max(0, -steps), min(count, count - steps))
    return lax.ppermute(value, axis, [(source, source + steps) for source in range(leading, last)])


def gelu_value(value):
    return 0.5 * value * (1.0 + jnp.tanh(GELU_ROOT * (value + GELU_CUBIC * value * value * value)))


def gelu_slope(value):
    inner = jnp.tanh(GELU_ROOT * (value + GELU_CUBIC * value * value * value))
    return 0.5 * (1.0 + inner) + 0.5 * value * (1.0 - inner * inner) * GELU_ROOT * (
        1.0 + 3.0 * GELU_CUBIC * value * value
    )


def norm_forward(token_rows, gain, shift):
    mean_row = jnp.mean(token_rows, axis=-1, keepdims=True)
    centred = token_rows - mean_row
    inverse = lax.rsqrt(jnp.mean(centred * centred, axis=-1, keepdims=True) + NORM_EPS)
    normed = centred * inverse
    return (normed * gain + shift, normed, inverse)


def norm_backward(grad_normed, normed, inverse, gain):
    scaled = grad_normed * gain
    inner = (
        scaled
        - jnp.mean(scaled, axis=-1, keepdims=True)
        - normed * jnp.mean(scaled * normed, axis=-1, keepdims=True)
    )
    return (inverse * inner, jnp.sum(grad_normed * normed, axis=0), jnp.sum(grad_normed, axis=0))


def layer_forward(layer_input, weights, qv_bias, up_bias):
    qkv_weight, out_weight, up_weight, down_weight, gains, shifts = weights
    image_count, seq_len, model_width = layer_input.shape
    local_heads = qkv_weight.shape[2] // HD
    score_scale = HD ** (-0.5)
    gain_rows = gains.astype(jnp.float32)
    shift_rows = shifts.astype(jnp.float32)
    token_rows = layer_input.astype(jnp.float32).reshape(-1, model_width)
    normed_one = norm_forward(token_rows, gain_rows[0], shift_rows[0])[0].astype(jnp.bfloat16)
    projected = jnp.einsum(
        "td,cde->cte", normed_one, qkv_weight, preferred_element_type=jnp.float32
    )
    bias_rows = qv_bias.astype(jnp.float32)
    queries = (projected[0] + bias_rows[0]).astype(jnp.bfloat16)
    key_rows = projected[1].astype(jnp.bfloat16)
    values = (projected[2] + bias_rows[1]).astype(jnp.bfloat16)
    head_shape = (image_count, seq_len, local_heads, HD)
    scores = (
        jnp.einsum(
            "bqhd,bkhd->bhqk",
            queries.reshape(head_shape),
            key_rows.reshape(head_shape),
            preferred_element_type=jnp.float32,
        )
        * score_scale
    )
    row_max = jnp.max(scores, axis=-1, keepdims=True)
    exp_scores = jnp.exp(scores - row_max)
    row_total = jnp.sum(exp_scores, axis=-1, keepdims=True)
    attn_probs = (exp_scores / row_total).astype(jnp.bfloat16)
    log_total = row_max + jnp.log(row_total)
    context = jnp.einsum(
        "bhqk,bkhd->bqhd",
        attn_probs,
        values.reshape(head_shape),
        preferred_element_type=jnp.float32,
    )
    context = context.astype(jnp.bfloat16).reshape(-1, local_heads * HD)
    attn_term = jnp.dot(context, out_weight, preferred_element_type=jnp.float32)
    hidden = token_rows + lax.psum(attn_term, "tensor") + shift_rows[1]
    normed_two = norm_forward(hidden, gain_rows[1], shift_rows[2])[0].astype(jnp.bfloat16)
    pre_act = jnp.dot(normed_two, up_weight, preferred_element_type=jnp.float32) + up_bias.astype(
        jnp.float32
    )
    active = gelu_value(pre_act).astype(jnp.bfloat16)
    mlp_term = jnp.dot(active, down_weight, preferred_element_type=jnp.float32)
    output_low = (hidden + lax.psum(mlp_term, "tensor") + shift_rows[3]).astype(jnp.bfloat16)
    stored = (
        layer_input,
        normed_one,
        queries,
        key_rows,
        values,
        log_total,
        context,
        hidden,
        normed_two,
        pre_act,
        active,
    )
    return (output_low, stored)


def layer_backward(grad_output, stored, weights):
    qkv_weight, out_weight, up_weight, down_weight, gains, shifts = weights
    (
        layer_input,
        normed_one,
        queries,
        key_rows,
        values,
        log_total,
        context,
        hidden,
        normed_two,
        pre_act,
        active,
    ) = stored
    image_count, seq_len, model_width = layer_input.shape
    local_heads = qkv_weight.shape[2] // HD
    score_scale = HD ** (-0.5)
    gain_rows = gains.astype(jnp.float32)
    shift_rows = shifts.astype(jnp.float32)
    grad_mix = grad_output.astype(jnp.bfloat16)
    grad_down = jnp.einsum("tf,td->fd", active, grad_mix, preferred_element_type=jnp.float32)
    grad_active = jnp.einsum("td,fd->tf", grad_mix, down_weight, preferred_element_type=jnp.float32)
    grad_pre = (grad_active * gelu_slope(pre_act)).astype(jnp.bfloat16)
    grad_up = jnp.einsum("td,tf->df", normed_two, grad_pre, preferred_element_type=jnp.float32)
    up_bias_grad = jnp.sum(grad_pre.astype(jnp.float32), axis=0)
    two_term = jnp.einsum("tf,df->td", grad_pre, up_weight, preferred_element_type=jnp.float32)
    centred_two, inverse_two = norm_forward(hidden, gain_rows[1], shift_rows[2])[1:]
    grad_normed_two = lax.psum(two_term, "tensor")
    from_two, gain_two_grad, shift_two_grad = norm_backward(
        grad_normed_two, centred_two, inverse_two, gain_rows[1]
    )
    grad_hidden = grad_output + from_two
    grad_attn = grad_hidden.astype(jnp.bfloat16)
    attn_shift_grad = jnp.sum(grad_attn.astype(jnp.float32), axis=0)
    mix_shift_grad = jnp.sum(grad_mix.astype(jnp.float32), axis=0)
    grad_out = jnp.einsum("te,td->ed", context, grad_attn, preferred_element_type=jnp.float32)
    grad_context = jnp.einsum(
        "td,ed->te", grad_attn, out_weight, preferred_element_type=jnp.float32
    ).astype(jnp.bfloat16)
    head_shape = (image_count, seq_len, local_heads, HD)
    query_heads = queries.reshape(head_shape)
    key_heads = key_rows.reshape(head_shape)
    value_heads = values.reshape(head_shape)
    context_grads = grad_context.reshape(head_shape)
    scores = (
        jnp.einsum("bqhd,bkhd->bhqk", query_heads, key_heads, preferred_element_type=jnp.float32)
        * score_scale
    )
    probs_full = jnp.exp(scores - log_total)
    mixed = jnp.einsum(
        "bqhd,bkhd->bhqk", context_grads, value_heads, preferred_element_type=jnp.float32
    )
    row_delta = jnp.sum(mixed * probs_full, axis=-1, keepdims=True)
    grad_scores = (probs_full * (mixed - row_delta)).astype(jnp.bfloat16)
    grad_values = jnp.einsum(
        "bhqk,bqhd->bkhd",
        probs_full.astype(jnp.bfloat16),
        context_grads,
        preferred_element_type=jnp.float32,
    ).astype(jnp.bfloat16)
    grad_queries = (
        jnp.einsum("bhqk,bkhd->bqhd", grad_scores, key_heads, preferred_element_type=jnp.float32)
        * score_scale
    ).astype(jnp.bfloat16)
    grad_keys = (
        jnp.einsum("bhqk,bqhd->bkhd", grad_scores, query_heads, preferred_element_type=jnp.float32)
        * score_scale
    ).astype(jnp.bfloat16)
    flat_shape = (-1, local_heads * HD)
    grad_proj = jnp.stack(
        [
            grad_queries.reshape(flat_shape),
            grad_keys.reshape(flat_shape),
            grad_values.reshape(flat_shape),
        ]
    )
    grad_qkv = jnp.einsum("td,cte->cde", normed_one, grad_proj, preferred_element_type=jnp.float32)
    qv_bias_grad = jnp.stack(
        [
            jnp.sum(grad_proj[0].astype(jnp.float32), axis=0),
            jnp.sum(grad_proj[2].astype(jnp.float32), axis=0),
        ]
    )
    one_term = jnp.einsum("cte,cde->td", grad_proj, qkv_weight, preferred_element_type=jnp.float32)
    token_rows = layer_input.astype(jnp.float32).reshape(-1, model_width)
    grad_normed_one = lax.psum(one_term, "tensor")
    centred_one, inverse_one = norm_forward(token_rows, gain_rows[0], shift_rows[0])[1:]
    from_one, gain_one_grad, shift_one_grad = norm_backward(
        grad_normed_one, centred_one, inverse_one, gain_rows[0]
    )
    grad_low = (grad_hidden + from_one).astype(jnp.bfloat16)
    grad_gains = jnp.stack([gain_one_grad, gain_two_grad])
    grad_shifts = jnp.stack([shift_one_grad, attn_shift_grad, shift_two_grad, mix_shift_grad])
    return (
        grad_low,
        (grad_qkv, grad_out, grad_up, grad_down, grad_gains, grad_shifts),
        (qv_bias_grad, up_bias_grad),
    )


def per_device(
    images,
    cotangent,
    qkv_weight,
    qv_bias,
    out_weight,
    up_weight,
    up_bias,
    down_weight,
    gains,
    shifts,
):
    micro_count, image_count, seq_len, model_width = images.shape
    section_index = lax.axis_index("section")
    local_qv = qv_bias[0]
    local_up = up_bias[0]
    weights = (
        lax.all_gather(qkv_weight[0], "fsdp", axis=1, tiled=True),
        lax.all_gather(out_weight[0], "fsdp", axis=1, tiled=True),
        lax.all_gather(up_weight[0], "fsdp", axis=0, tiled=True),
        lax.all_gather(down_weight[0], "fsdp", axis=1, tiled=True),
        lax.all_gather(gains[0], "fsdp", axis=1, tiled=True),
        lax.all_gather(shifts[0], "fsdp", axis=1, tiled=True),
    )

    def forward_tick(carried, tick_index):
        own_input = lax.dynamic_index_in_dim(
            images, jnp.minimum(tick_index, micro_count - 1), 0, keepdims=False
        )
        layer_input = jnp.where(section_index == 0, own_input, carried)
        output_low, stored = layer_forward(layer_input, weights, local_qv, local_up)
        output_low = output_low.reshape(image_count, seq_len, model_width)
        passed = from_behind(output_low, "section", 1)
        return (passed, (output_low, stored))

    ticks = jnp.arange(micro_count + 1, dtype=jnp.int32)
    output_all, stored_all = lax.scan(forward_tick, jnp.zeros_like(images[0]), ticks)[1]
    section_outputs = lax.dynamic_slice_in_dim(output_all, section_index, micro_count, 0)
    start_sums = tuple((jnp.zeros(item.shape, jnp.float32) for item in weights))
    start_biases = (jnp.zeros(local_qv.shape, jnp.float32), jnp.zeros(local_up.shape, jnp.float32))

    def backward_tick(carry, tick_index):
        received, grad_sums, bias_totals = carry
        micro_index = micro_count - tick_index - section_index
        is_valid = (micro_index >= 0) & (micro_index < micro_count)
        safe_index = jnp.clip(micro_index, 0, micro_count - 1)
        own_grad = (
            lax.dynamic_index_in_dim(cotangent, safe_index, 0, keepdims=False)
            .astype(jnp.float32)
            .reshape(-1, model_width)
        )
        grad_output = jnp.where(section_index == 1, own_grad, received)
        stored = tuple(
            (
                lax.dynamic_index_in_dim(item, safe_index + section_index, 0, keepdims=False)
                for item in stored_all
            )
        )
        grad_low, grads, biases = layer_backward(grad_output, stored, weights)
        grads = tuple((jnp.where(is_valid, item, 0.0) for item in grads))
        biases = tuple((jnp.where(is_valid, item, 0.0) for item in biases))
        grad_low = grad_low.reshape(image_count, seq_len, model_width)
        passed = from_behind(grad_low, "section", -1).astype(jnp.float32).reshape(-1, model_width)
        grad_sums = tuple((first + second for first, second in zip(grad_sums, grads)))
        bias_totals = tuple((first + second for first, second in zip(bias_totals, biases)))
        return ((passed, grad_sums, bias_totals), grad_low)

    start_grad = jnp.zeros((image_count * seq_len, model_width), jnp.float32)
    finished, grad_all = lax.scan(backward_tick, (start_grad, start_sums, start_biases), ticks)
    grad_sums, bias_totals = (finished[1], finished[2])
    final_grads = (
        lax.psum_scatter(
            grad_sums[0].astype(jnp.bfloat16), "fsdp", scatter_dimension=1, tiled=True
        ).astype(jnp.float32),
        lax.psum_scatter(
            grad_sums[1].astype(jnp.bfloat16), "fsdp", scatter_dimension=1, tiled=True
        ).astype(jnp.float32),
        lax.psum_scatter(
            grad_sums[2].astype(jnp.bfloat16), "fsdp", scatter_dimension=0, tiled=True
        ).astype(jnp.float32),
        lax.psum_scatter(
            grad_sums[3].astype(jnp.bfloat16), "fsdp", scatter_dimension=1, tiled=True
        ).astype(jnp.float32),
        lax.psum_scatter(
            grad_sums[4].astype(jnp.bfloat16), "fsdp", scatter_dimension=1, tiled=True
        ).astype(jnp.float32),
        lax.psum_scatter(
            grad_sums[5].astype(jnp.bfloat16), "fsdp", scatter_dimension=1, tiled=True
        ).astype(jnp.float32),
    )
    final_biases = lax.psum((bias_totals[0], bias_totals[1]), "fsdp")
    gain_grads, shift_grads = (final_grads[4], final_grads[5])
    input_grads = jnp.flip(lax.dynamic_slice_in_dim(grad_all, 1 - section_index, micro_count, 0), 0)
    return (
        section_outputs[None],
        input_grads[None],
        final_grads[0][None],
        final_biases[0][None],
        final_grads[1][None],
        final_grads[2][None],
        final_biases[1][None],
        final_grads[3][None],
        gain_grads[None],
        shift_grads[None],
    )


def solution(mesh):
    return jax.shard_map(
        per_device,
        mesh=mesh,
        in_specs=(
            P(None, "fsdp", None, None),
            P(None, "fsdp", None, None),
            P("section", None, "fsdp", "tensor"),
            P("section", None, "tensor"),
            P("section", "tensor", "fsdp"),
            P("section", "fsdp", "tensor"),
            P("section", "tensor"),
            P("section", "tensor", "fsdp"),
            P("section", None, "fsdp"),
            P("section", None, "fsdp"),
        ),
        out_specs=(
            P("section", None, "fsdp", None, None),
            P("section", None, "fsdp", None, None),
            P("section", None, "fsdp", "tensor"),
            P("section", None, "tensor"),
            P("section", "tensor", "fsdp"),
            P("section", "fsdp", "tensor"),
            P("section", "tensor"),
            P("section", "tensor", "fsdp"),
            P("section", None, "fsdp"),
            P("section", None, "fsdp"),
        ),
        check_vma=False,
    )
```

profile of v0, /device:TPU:0, one launch (start us, length us, event | category | flops | bytes accessed | tf_op | source)
XLA Modules:
  0.0 2444.3 jit_solution(16826438468239682339)
XLA Ops:
  12.3 19.3 all-gather.3
  35.5 12.4 all-gather
  51.0 8.1 all-gather.1
  65.6 7.1 copy.121
  72.7 6.0 all-gather.14.cloned.1.call-done
  78.7 5.1 copy.122
  83.8 22.2 all-gather.12.cloned.1.call-done
  112.5 1034.5 %while.66 = (s32[]{:T(128)}, bf16[1,729,1152]{2,1,0:T(8,128)(2,1)}, bf16[3,1,729,1152]{3,2,1,0:T(8,128)(2,1)}, bf16[3,1,729,1152]{3,2,1,0:T(8,128)(2,1)}, bf16[3...) while((s32[]{:T(128)}, bf16[1,729,1152]{2,1,0:T(8,128)(2,1)}, ...), condition=%wide.region_9.10_spmd, body=%wide.region_0.9_spmd.sunk | while | flops 6232035840 | bytes 263704656 | solution.py:247
  145.6 130.7 %all-reduce.6.cloned.1.call-done = f32[729,1152]{1,0:T(8,128)} async-done(((f32[729,1152]{1,0:T(8,128)}), f32[729,1152]{1,0:T(8,128)}) %all-reduce.6.cloned.1.call-update) | async-done | bytes 3359248 | tf_op jit(solution)/shard_map/while/body/eval_jaxpr/psum | solution.py:86
  276.3 4.6 bitcast_dynamic-update-slice_fusion.17
  297.6 124.3 %all-reduce.8.cloned.1.call-done = f32[729,1152]{1,0:T(8,128)} async-done(((f32[729,1152]{1,0:T(8,128)}), f32[729,1152]{1,0:T(8,128)}) %all-reduce.8.cloned.1.call-update) | async-done | bytes 3359248 | tf_op jit(solution)/shard_map/while/body/eval_jaxpr/psum | solution.py:93
  426.2 4.6 collective-permute-start
  436.2 29.8 %collective-permute-done = bf16[1,729,1152]{2,1,0:T(8,128)(2,1)} collective-permute-done((bf16[1,729,1152]{2,1,0:T(8,128)(2,1)}, bf16[1,729,1152]{2,1,0:T(8,128)(2,1)}, u32[]{:S(2)}, u32[]{:S(2)}) %collective-permute-start) | collective-permute-done | bytes 1679648 | tf_op jit(solution)/shard_map/while/body/eval_jaxpr/ppermute | solution.py:15
  486.1 130.8 %all-reduce.6.cloned.1.call-done = f32[729,1152]{1,0:T(8,128)} async-done(((f32[729,1152]{1,0:T(8,128)}), f32[729,1152]{1,0:T(8,128)}) %all-reduce.6.cloned.1.call-update) | async-done | bytes 3359248 | tf_op jit(solution)/shard_map/while/body/eval_jaxpr/psum | solution.py:86
  616.9 4.7 bitcast_dynamic-update-slice_fusion.17
  638.1 124.4 %all-reduce.8.cloned.1.call-done = f32[729,1152]{1,0:T(8,128)} async-done(((f32[729,1152]{1,0:T(8,128)}), f32[729,1152]{1,0:T(8,128)}) %all-reduce.8.cloned.1.call-update) | async-done | bytes 3359248 | tf_op jit(solution)/shard_map/while/body/eval_jaxpr/psum | solution.py:93
  766.7 4.6 collective-permute-start
  776.8 29.7 %collective-permute-done = bf16[1,729,1152]{2,1,0:T(8,128)(2,1)} collective-permute-done((bf16[1,729,1152]{2,1,0:T(8,128)(2,1)}, bf16[1,729,1152]{2,1,0:T(8,128)(2,1)}, u32[]{:S(2)}, u32[]{:S(2)}) %collective-permute-start) | collective-permute-done | bytes 1679648 | tf_op jit(solution)/shard_map/while/body/eval_jaxpr/ppermute | solution.py:15
  826.6 130.8 %all-reduce.6.cloned.1.call-done = f32[729,1152]{1,0:T(8,128)} async-done(((f32[729,1152]{1,0:T(8,128)}), f32[729,1152]{1,0:T(8,128)}) %all-reduce.6.cloned.1.call-update) | async-done | bytes 3359248 | tf_op jit(solution)/shard_map/while/body/eval_jaxpr/psum | solution.py:86
  957.4 4.7 bitcast_dynamic-update-slice_fusion.17
  978.7 124.3 %all-reduce.8.cloned.1.call-done = f32[729,1152]{1,0:T(8,128)} async-done(((f32[729,1152]{1,0:T(8,128)}), f32[729,1152]{1,0:T(8,128)}) %all-reduce.8.cloned.1.call-update) | async-done | bytes 3359248 | tf_op jit(solution)/shard_map/while/body/eval_jaxpr/psum | solution.py:93
  1107.1 4.6 collective-permute-start
  1117.1 29.7 %collective-permute-done = bf16[1,729,1152]{2,1,0:T(8,128)(2,1)} collective-permute-done((bf16[1,729,1152]{2,1,0:T(8,128)(2,1)}, bf16[1,729,1152]{2,1,0:T(8,128)(2,1)}, u32[]{:S(2)}, u32[]{:S(2)}) %collective-permute-start) | collective-permute-done | bytes 1679648 | tf_op jit(solution)/shard_map/while/body/eval_jaxpr/ppermute | solution.py:15
  1149.9 1104.1 %while.67 = (s32[]{:T(128)}, f32[729,1152]{1,0:T(8,128)S(1)}, f32[3,1152,288]{1,2,0:T(8,128)}, f32[288,1152]{1,0:T(8,128)}, f32[1152,1076]{0,1:T(8,128)}, /*inde...) while((s32[]{:T(128)}, f32[729,1152]{1,0:T(8,128)S(1)}, ...), condition=%wide.region_31.32_spmd.clone, body=%wide.region_10.31_spmd.clone.sunk | while | flops 12738733056 | bytes 490833920 | solution.py:279
  1175.0 6.1 convert_reduce_fusion.16
  1195.7 4.9 fusion.210
  1200.5 115.7 %all-reduce.10.cloned.1.call-done = f32[729,1152]{1,0:T(8,128)} async-done(((f32[729,1152]{1,0:T(8,128)}), f32[729,1152]{1,0:T(8,128)}) %all-reduce.10.cloned.1.call-update) | async-done | bytes 3359248 | tf_op jit(solution)/shard_map/while/body/eval_jaxpr/psum | solution.py:138
  1316.2 4.5 multiply_reduce_fusion.16
  1327.0 4.7 multiply_reduce_fusion.17
  1331.7 10.2 multiply_convert_fusion.2
  1347.2 5.5 convert_reduce_fusion.18
  1361.9 6.2 fusion.215
  1368.2 5.2 fusion.216
  1378.7 106.2 %all-reduce.12.cloned.1.call-done = f32[729,1152]{1,0:T(8,128)} async-done(((f32[729,1152]{1,0:T(8,128)}), f32[729,1152]{1,0:T(8,128)}) %all-reduce.12.cloned.1.call-update) | async-done | bytes 3359248 | tf_op jit(solution)/shard_map/while/body/eval_jaxpr/psum | solution.py:196
  1498.5 34.7 %collective-permute-done.1 = bf16[1,729,1152]{2,1,0:T(8,128)(2,1)S(1)} collective-permute-done((bf16[1,729,1152]{2,1,0:T(8,128)(2,1)S(1)}, bf16[1,729,1152]{2,1,0:T(8,128)(2,1)S(1)}, u32[]{:S(2)}, u32[]{:S(2)}) %collective-permute-start.1) | collective-permute-done | bytes 1679648 | tf_op jit(solution)/shard_map/while/body/eval_jaxpr/ppermute | solution.py:15
  1537.1 6.1 convert_reduce_fusion.16
  1557.9 4.9 fusion.210
  1562.8 113.6 %all-reduce.10.cloned.1.call-done = f32[729,1152]{1,0:T(8,128)} async-done(((f32[729,1152]{1,0:T(8,128)}), f32[729,1152]{1,0:T(8,128)}) %all-reduce.10.cloned.1.call-update) | async-done | bytes 3359248 | tf_op jit(solution)/shard_map/while/body/eval_jaxpr/psum | solution.py:138
  1676.4 4.5 multiply_reduce_fusion.16
  1687.2 4.7 multiply_reduce_fusion.17
  1691.9 10.2 multiply_convert_fusion.2
  1707.4 5.5 convert_reduce_fusion.18
  1722.2 7.7 fusion.215
  1729.9 5.2 fusion.216
  1740.9 104.2 %all-reduce.12.cloned.1.call-done = f32[729,1152]{1,0:T(8,128)} async-done(((f32[729,1152]{1,0:T(8,128)}), f32[729,1152]{1,0:T(8,128)}) %all-reduce.12.cloned.1.call-update) | async-done | bytes 3359248 | tf_op jit(solution)/shard_map/while/body/eval_jaxpr/psum | solution.py:196
  1858.7 34.7 %collective-permute-done.1 = bf16[1,729,1152]{2,1,0:T(8,128)(2,1)S(1)} collective-permute-done((bf16[1,729,1152]{2,1,0:T(8,128)(2,1)S(1)}, bf16[1,729,1152]{2,1,0:T(8,128)(2,1)S(1)}, u32[]{:S(2)}, u32[]{:S(2)}) %collective-permute-start.1) | collective-permute-done | bytes 1679648 | tf_op jit(solution)/shard_map/while/body/eval_jaxpr/ppermute | solution.py:15
  1897.3 6.1 convert_reduce_fusion.16
  1918.1 4.9 fusion.210
  1922.9 113.6 %all-reduce.10.cloned.1.call-done = f32[729,1152]{1,0:T(8,128)} async-done(((f32[729,1152]{1,0:T(8,128)}), f32[729,1152]{1,0:T(8,128)}) %all-reduce.10.cloned.1.call-update) | async-done | bytes 3359248 | tf_op jit(solution)/shard_map/while/body/eval_jaxpr/psum | solution.py:138
  2047.2 4.7 multiply_reduce_fusion.17
  2051.8 10.2 multiply_convert_fusion.2
  2067.4 5.5 convert_reduce_fusion.18
  2082.2 7.7 fusion.215
  2089.9 5.2 fusion.216
  2100.9 104.2 %all-reduce.12.cloned.1.call-done = f32[729,1152]{1,0:T(8,128)} async-done(((f32[729,1152]{1,0:T(8,128)}), f32[729,1152]{1,0:T(8,128)}) %all-reduce.12.cloned.1.call-update) | async-done | bytes 3359248 | tf_op jit(solution)/shard_map/while/body/eval_jaxpr/psum | solution.py:196
  2218.7 34.7 %collective-permute-done.1 = bf16[1,729,1152]{2,1,0:T(8,128)(2,1)S(1)} collective-permute-done((bf16[1,729,1152]{2,1,0:T(8,128)(2,1)S(1)}, bf16[1,729,1152]{2,1,0:T(8,128)(2,1)S(1)}, u32[]{:S(2)}, u32[]{:S(2)}) %collective-permute-start.1) | collective-permute-done | bytes 1679648 | tf_op jit(solution)/shard_map/while/body/eval_jaxpr/ppermute | solution.py:15
  2262.4 6.0 copy.137
  2285.4 6.0 copy.129
  2291.3 5.2 constant_dynamic-slice_fusion.3
  2296.5 31.6 %rev.4 = bf16[2,1,729,1152]{3,0,2,1:T(2,128)(2,1)} reverse(bf16[2,1,729,1152]{3,0,2,1:T(2,128)(2,1)} %constant_dynamic-slice_fusion.3), dimensions={0} | reverse | bytes 6718464 | tf_op jit(solution)/shard_map/jit(_flip)/rev | solution.py:303
  2334.8 6.5 all-reduce
  2346.4 13.1 reduce-scatter.19.cloned.1.call-done
  2364.7 32.0 %reduce-scatter.23.cloned.1.call-done = bf16[288,1076]{1,0:T(8,128)(2,1)} async-done(((bf16[1152,1076]{1,0:T(8,128)(2,1)}), bf16[288,1076]{1,0:T(8,128)(2,1)}) %reduce-scatter.23.cloned.1.call-update) | async-done | bytes 619792
  2399.9 34.1 %reduce-scatter.25.cloned.1.call-done = bf16[288,1076]{1,0:T(8,128)(2,1)} async-done(((bf16[1152,1076]{1,0:T(8,128)(2,1)}), bf16[288,1076]{1,0:T(8,128)(2,1)}) %reduce-scatter.25.cloned.1.call-update) | async-done | bytes 619792
  (758 shorter events, 388.6 us)
Async XLA Ops:
  7.2 58.4 %all-gather.10.cloned.1.call-start = ((), (), s32[]{:S(2)}) async-start(), calls=%async_computation.6 | async-start | bytes 4423680 | tf_op jit(solution)/shard_map/all_gather | solution.py:228
  9.8 25.6 %copy-start.65 = (bf16[1,2,288]{2,1,0:T(2,128)(2,1)S(1)}, bf16[1,2,288]{2,1,0:T(2,128)(2,1)}, u32[]{:S(2)}) copy-start(bf16[1,2,288]{2,1,0:T(2,128)(2,1)} %param.22) | copy-start | bytes 3460
  9.8 68.9 %all-gather.14.cloned.1.call-start = ((), (), s32[]{:S(2)}) async-start(), calls=%async_computation.8 | async-start | bytes 3317760 | tf_op jit(solution)/shard_map/all_gather | solution.py:231
  10.5 95.4 %all-gather.12.cloned.1.call-start = ((), (), s32[]{:S(2)}) async-start(), calls=%async_computation.7 | async-start | bytes 3317760 | tf_op jit(solution)/shard_map/all_gather | solution.py:230
  125.5 150.8 %all-reduce.6.cloned.1.call-start = ((), (), s32[]{:S(2)}) async-start(), calls=%async_computation.15 | async-start | bytes 6782976 | tf_op jit(solution)/shard_map/while/body/eval_jaxpr/psum | solution.py:86
  142.6 133.7 %copy-start.42 = (f32[1152]{0:T(1024)S(1)}, f32[1152]{0:T(1024)}, u32[]{:S(2)}) copy-start(f32[1152]{0:T(1024)} %get-tuple-element.1532) | copy-start | bytes 13828 | tf_op jit(solution)/shard_map/while
  145.5 276.4 %all-reduce.8.cloned.1.call-start = ((), (), s32[]{:S(2)}) async-start(), calls=%async_computation.16 | async-start | bytes 6782976 | tf_op jit(solution)/shard_map/while/body/eval_jaxpr/psum | solution.py:93
  293.6 128.4 %copy-start.43 = (f32[1152]{0:T(1024)S(1)}, f32[1152]{0:T(1024)}, u32[]{:S(2)}) copy-start(f32[1152]{0:T(1024)} %get-tuple-element.1531) | copy-start | bytes 13828 | tf_op jit(solution)/shard_map/while
  421.9 8.8 copy-start.21
  426.2 39.8 %collective-permute-start = (bf16[1,729,1152]{2,1,0:T(8,128)(2,1)}, bf16[1,729,1152]{2,1,0:T(8,128)(2,1)}, u32[]{:S(2)}, u32[]{:S(2)}) collective-permute-start(bf16[1,729,1152]{2,1,0:T(8,128)(2,1)} %bitcast.319), channel_id=1, source_target_pairs={{0,16},{1,17},{2,18},{3,19},{4,20},{5,21},{6,22},{7,23},{8,24},{9,... | collective-permute-start | bytes 5038856 | tf_op jit(solution)/shard_map/while/body/eval_jaxpr/ppermute | solution.py:15
  433.9 32.0 %copy-start.29 = (bf16[2,1,729,1152]{3,2,1,0:T(8,128)(2,1)S(1)}, bf16[2,1,729,1152]{3,2,1,0:T(8,128)(2,1)}, u32[]{:S(2)}) copy-start(bf16[2,1,729,1152]{3,2,1,0:T(8,128)(2,1)} %copy-done.28) | copy-start | bytes 10077700 | tf_op jit(solution)/shard_map/while
  433.9 32.0 %copy-start.46 = (bf16[2,1152]{1,0:T(2,128)(2,1)S(1)}, bf16[2,1152]{1,0:T(2,128)(2,1)}, u32[]{:S(2)}) copy-start(bf16[2,1152]{1,0:T(2,128)(2,1)} %copy-done.45) | copy-start | bytes 13828 | tf_op jit(solution)/shard_map/while
  433.9 32.0 %copy-start.51 = (bf16[4,1152]{1,0:T(4,128)(2,1)S(1)}, bf16[4,1152]{1,0:T(4,128)(2,1)}, u32[]{:S(2)}) copy-start(bf16[4,1152]{1,0:T(4,128)(2,1)} %copy-done.50) | copy-start | bytes 27652 | tf_op jit(solution)/shard_map/while
  433.9 32.0 %copy-start.61 = (bf16[1,2,288]{2,1,0:T(2,128)(2,1)S(1)}, bf16[1,2,288]{2,1,0:T(2,128)(2,1)}, u32[]{:S(2)}) copy-start(bf16[1,2,288]{2,1,0:T(2,128)(2,1)} %get-tuple-element.1899) | copy-start | bytes 3460 | tf_op jit(solution)/shard_map/while
  433.9 32.0 %copy-start.69 = (s32[3]{0:T(128)S(1)}, s32[3]{0:T(128)}, u32[]{:S(2)}) copy-start(s32[3]{0:T(128)} %copy-done.68) | copy-start | bytes 40 | tf_op jit(solution)/shard_map/while
  466.0 150.8 %all-reduce.6.cloned.1.call-start = ((), (), s32[]{:S(2)}) async-start(), calls=%async_computation.15 | async-start | bytes 6782976 | tf_op jit(solution)/shard_map/while/body/eval_jaxpr/psum | solution.py:86
  483.1 133.8 %copy-start.42 = (f32[1152]{0:T(1024)S(1)}, f32[1152]{0:T(1024)}, u32[]{:S(2)}) copy-start(f32[1152]{0:T(1024)} %get-tuple-element.1532) | copy-start | bytes 13828 | tf_op jit(solution)/shard_map/while
  486.0 276.4 %all-reduce.8.cloned.1.call-start = ((), (), s32[]{:S(2)}) async-start(), calls=%async_computation.16 | async-start | bytes 6782976 | tf_op jit(solution)/shard_map/while/body/eval_jaxpr/psum | solution.py:93
  634.1 128.4 %copy-start.43 = (f32[1152]{0:T(1024)S(1)}, f32[1152]{0:T(1024)}, u32[]{:S(2)}) copy-start(f32[1152]{0:T(1024)} %get-tuple-element.1531) | copy-start | bytes 13828 | tf_op jit(solution)/shard_map/while
  762.4 8.8 copy-start.21
  766.7 39.8 %collective-permute-start = (bf16[1,729,1152]{2,1,0:T(8,128)(2,1)}, bf16[1,729,1152]{2,1,0:T(8,128)(2,1)}, u32[]{:S(2)}, u32[]{:S(2)}) collective-permute-start(bf16[1,729,1152]{2,1,0:T(8,128)(2,1)} %bitcast.319), channel_id=1, source_target_pairs={{0,16},{1,17},{2,18},{3,19},{4,20},{5,21},{6,22},{7,23},{8,24},{9,... | collective-permute-start | bytes 5038856 | tf_op jit(solution)/shard_map/while/body/eval_jaxpr/ppermute | solution.py:15
  774.5 32.0 %copy-start.29 = (bf16[2,1,729,1152]{3,2,1,0:T(8,128)(2,1)S(1)}, bf16[2,1,729,1152]{3,2,1,0:T(8,128)(2,1)}, u32[]{:S(2)}) copy-start(bf16[2,1,729,1152]{3,2,1,0:T(8,128)(2,1)} %copy-done.28) | copy-start | bytes 10077700 | tf_op jit(solution)/shard_map/while
  774.5 32.0 %copy-start.46 = (bf16[2,1152]{1,0:T(2,128)(2,1)S(1)}, bf16[2,1152]{1,0:T(2,128)(2,1)}, u32[]{:S(2)}) copy-start(bf16[2,1152]{1,0:T(2,128)(2,1)} %copy-done.45) | copy-start | bytes 13828 | tf_op jit(solution)/shard_map/while
  774.5 32.0 %copy-start.51 = (bf16[4,1152]{1,0:T(4,128)(2,1)S(1)}, bf16[4,1152]{1,0:T(4,128)(2,1)}, u32[]{:S(2)}) copy-start(bf16[4,1152]{1,0:T(4,128)(2,1)} %copy-done.50) | copy-start | bytes 27652 | tf_op jit(solution)/shard_map/while
  774.5 32.0 %copy-start.61 = (bf16[1,2,288]{2,1,0:T(2,128)(2,1)S(1)}, bf16[1,2,288]{2,1,0:T(2,128)(2,1)}, u32[]{:S(2)}) copy-start(bf16[1,2,288]{2,1,0:T(2,128)(2,1)} %get-tuple-element.1899) | copy-start | bytes 3460 | tf_op jit(solution)/shard_map/while
  774.5 32.0 %copy-start.69 = (s32[3]{0:T(128)S(1)}, s32[3]{0:T(128)}, u32[]{:S(2)}) copy-start(s32[3]{0:T(128)} %copy-done.68) | copy-start | bytes 40 | tf_op jit(solution)/shard_map/while
  806.5 150.8 %all-reduce.6.cloned.1.call-start = ((), (), s32[]{:S(2)}) async-start(), calls=%async_computation.15 | async-start | bytes 6782976 | tf_op jit(solution)/shard_map/while/body/eval_jaxpr/psum | solution.py:86
  823.6 133.8 %copy-start.42 = (f32[1152]{0:T(1024)S(1)}, f32[1152]{0:T(1024)}, u32[]{:S(2)}) copy-start(f32[1152]{0:T(1024)} %get-tuple-element.1532) | copy-start | bytes 13828 | tf_op jit(solution)/shard_map/while
  826.5 276.4 %all-reduce.8.cloned.1.call-start = ((), (), s32[]{:S(2)}) async-start(), calls=%async_computation.16 | async-start | bytes 6782976 | tf_op jit(solution)/shard_map/while/body/eval_jaxpr/psum | solution.py:93
  974.6 128.4 %copy-start.43 = (f32[1152]{0:T(1024)S(1)}, f32[1152]{0:T(1024)}, u32[]{:S(2)}) copy-start(f32[1152]{0:T(1024)} %get-tuple-element.1531) | copy-start | bytes 13828 | tf_op jit(solution)/shard_map/while
  1103.0 8.7 copy-start.21
  1107.1 39.8 %collective-permute-start = (bf16[1,729,1152]{2,1,0:T(8,128)(2,1)}, bf16[1,729,1152]{2,1,0:T(8,128)(2,1)}, u32[]{:S(2)}, u32[]{:S(2)}) collective-permute-start(bf16[1,729,1152]{2,1,0:T(8,128)(2,1)} %bitcast.319), channel_id=1, source_target_pairs={{0,16},{1,17},{2,18},{3,19},{4,20},{5,21},{6,22},{7,23},{8,24},{9,... | collective-permute-start | bytes 5038856 | tf_op jit(solution)/shard_map/while/body/eval_jaxpr/ppermute | solution.py:15
  1114.9 32.0 %copy-start.29 = (bf16[2,1,729,1152]{3,2,1,0:T(8,128)(2,1)S(1)}, bf16[2,1,729,1152]{3,2,1,0:T(8,128)(2,1)}, u32[]{:S(2)}) copy-start(bf16[2,1,729,1152]{3,2,1,0:T(8,128)(2,1)} %copy-done.28) | copy-start | bytes 10077700 | tf_op jit(solution)/shard_map/while
  1114.9 32.0 %copy-start.46 = (bf16[2,1152]{1,0:T(2,128)(2,1)S(1)}, bf16[2,1152]{1,0:T(2,128)(2,1)}, u32[]{:S(2)}) copy-start(bf16[2,1152]{1,0:T(2,128)(2,1)} %copy-done.45) | copy-start | bytes 13828 | tf_op jit(solution)/shard_map/while
  1114.9 32.0 %copy-start.51 = (bf16[4,1152]{1,0:T(4,128)(2,1)S(1)}, bf16[4,1152]{1,0:T(4,128)(2,1)}, u32[]{:S(2)}) copy-start(bf16[4,1152]{1,0:T(4,128)(2,1)} %copy-done.50) | copy-start | bytes 27652 | tf_op jit(solution)/shard_map/while
  1114.9 32.0 %copy-start.61 = (bf16[1,2,288]{2,1,0:T(2,128)(2,1)S(1)}, bf16[1,2,288]{2,1,0:T(2,128)(2,1)}, u32[]{:S(2)}) copy-start(bf16[1,2,288]{2,1,0:T(2,128)(2,1)} %get-tuple-element.1899) | copy-start | bytes 3460 | tf_op jit(solution)/shard_map/while
  1114.9 32.0 %copy-start.69 = (s32[3]{0:T(128)S(1)}, s32[3]{0:T(128)}, u32[]{:S(2)}) copy-start(s32[3]{0:T(128)} %copy-done.68) | copy-start | bytes 40 | tf_op jit(solution)/shard_map/while
  1171.3 144.9 %all-reduce.10.cloned.1.call-start = ((), (), s32[]{:S(2)}) async-start(), calls=%async_computation.17 | async-start | bytes 6782976 | tf_op jit(solution)/shard_map/while/body/eval_jaxpr/psum | solution.py:138
  1175.0 7.4 copy-start.67
  1186.8 298.1 %all-reduce.12.cloned.1.call-start = ((), (), s32[]{:S(2)}) async-start(), calls=%async_computation.18 | async-start | bytes 6782976 | tf_op jit(solution)/shard_map/while/body/eval_jaxpr/psum | solution.py:196
  1357.5 10.6 slice-start.3
  1492.7 40.5 %collective-permute-start.1 = (bf16[1,729,1152]{2,1,0:T(8,128)(2,1)S(1)}, bf16[1,729,1152]{2,1,0:T(8,128)(2,1)S(1)}, u32[]{:S(2)}, u32[]{:S(2)}) collective-permute-start(bf16[1,729,1152]{2,1,0:T(8,128)(2,1)S(1)} %bitcast.382), channel_id=1, source_target_pairs={{16,0},{17,1},{18,2},{19,3},{20,4},{21,5},{22,6},{23,7},{24,8},{25... | collective-permute-start | bytes 5038856 | tf_op jit(solution)/shard_map/while/body/eval_jaxpr/ppermute | solution.py:15
  1498.4 35.0 %copy-start.33 = (f32[3,1152,288]{1,2,0:T(8,128)}, f32[3,1152,288]{1,2,0:T(8,128)S(1)}, u32[]{:S(2)}) copy-start(f32[3,1152,288]{1,2,0:T(8,128)S(1)} %bitcast_add_fusion.2) | copy-start | bytes 11943940 | tf_op jit(solution)/shard_map/while
  1533.4 143.0 %all-reduce.10.cloned.1.call-start = ((), (), s32[]{:S(2)}) async-start(), calls=%async_computation.17 | async-start | bytes 6782976 | tf_op jit(solution)/shard_map/while/body/eval_jaxpr/psum | solution.py:138
  1548.9 296.2 %all-reduce.12.cloned.1.call-start = ((), (), s32[]{:S(2)}) async-start(), calls=%async_computation.18 | async-start | bytes 6782976 | tf_op jit(solution)/shard_map/while/body/eval_jaxpr/psum | solution.py:196
  1717.7 12.1 slice-start.3
  1722.1 7.7 copy-start.27
  1722.1 7.7 slice-start.4
  1852.9 40.5 %collective-permute-start.1 = (bf16[1,729,1152]{2,1,0:T(8,128)(2,1)S(1)}, bf16[1,729,1152]{2,1,0:T(8,128)(2,1)S(1)}, u32[]{:S(2)}, u32[]{:S(2)}) collective-permute-start(bf16[1,729,1152]{2,1,0:T(8,128)(2,1)S(1)} %bitcast.382), channel_id=1, source_target_pairs={{16,0},{17,1},{18,2},{19,3},{20,4},{21,5},{22,6},{23,7},{24,8},{25... | collective-permute-start | bytes 5038856 | tf_op jit(solution)/shard_map/while/body/eval_jaxpr/ppermute | solution.py:15
  1858.6 35.0 %copy-start.33 = (f32[3,1152,288]{1,2,0:T(8,128)}, f32[3,1152,288]{1,2,0:T(8,128)S(1)}, u32[]{:S(2)}) copy-start(f32[3,1152,288]{1,2,0:T(8,128)S(1)} %bitcast_add_fusion.2) | copy-start | bytes 11943940 | tf_op jit(solution)/shard_map/while
  1893.6 143.0 %all-reduce.10.cloned.1.call-start = ((), (), s32[]{:S(2)}) async-start(), calls=%async_computation.17 | async-start | bytes 6782976 | tf_op jit(solution)/shard_map/while/body/eval_jaxpr/psum | solution.py:138
  1897.3 7.4 copy-start.67
  1909.1 296.0 %all-reduce.12.cloned.1.call-start = ((), (), s32[]{:S(2)}) async-start(), calls=%async_computation.18 | async-start | bytes 6782976 | tf_op jit(solution)/shard_map/while/body/eval_jaxpr/psum | solution.py:196
  2077.7 12.1 slice-start.3
  2082.1 7.7 copy-start.27
  2082.1 7.7 slice-start.4
  2212.9 40.5 %collective-permute-start.1 = (bf16[1,729,1152]{2,1,0:T(8,128)(2,1)S(1)}, bf16[1,729,1152]{2,1,0:T(8,128)(2,1)S(1)}, u32[]{:S(2)}, u32[]{:S(2)}) collective-permute-start(bf16[1,729,1152]{2,1,0:T(8,128)(2,1)S(1)} %bitcast.382), channel_id=1, source_target_pairs={{16,0},{17,1},{18,2},{19,3},{20,4},{21,5},{22,6},{23,7},{24,8},{25... | collective-permute-start | bytes 5038856 | tf_op jit(solution)/shard_map/while/body/eval_jaxpr/ppermute | solution.py:15
  2218.6 35.0 %copy-start.33 = (f32[3,1152,288]{1,2,0:T(8,128)}, f32[3,1152,288]{1,2,0:T(8,128)S(1)}, u32[]{:S(2)}) copy-start(f32[3,1152,288]{1,2,0:T(8,128)S(1)} %bitcast_add_fusion.2) | copy-start | bytes 11943940 | tf_op jit(solution)/shard_map/while
  2254.0 87.3 %reduce-scatter.27.cloned.1.call-start = ((), (), s32[]{:S(2)}) async-start(), calls=%async_computation.13 | async-start | bytes 368640
  2255.0 87.9 %reduce-scatter.29.cloned.1.call-start = ((), (), s32[]{:S(2)}) async-start(), calls=%async_computation.14 | async-start | bytes 368640
  2256.0 88.4 %reduce-scatter.21.cloned.1.call-start = ((), (), s32[]{:S(2)}) async-start(), calls=%async_computation.10 | async-start | bytes 1105920
  2258.7 100.9 %reduce-scatter.19.cloned.1.call-start = ((), (), s32[]{:S(2)}) async-start(), calls=%async_computation.9 | async-start | bytes 2580480
  2272.6 124.2 %reduce-scatter.23.cloned.1.call-start = ((), (), s32[]{:S(2)}) async-start(), calls=%async_computation.11 | async-start | bytes 3317760
  2278.6 155.4 %reduce-scatter.25.cloned.1.call-start = ((), (), s32[]{:S(2)}) async-start(), calls=%async_computation.12 | async-start | bytes 3317760
  (170 other events, 567.4 us)
Sparse Core Ops, SparseCore 0:
  10.1 40.3 all-gather.9
  52.1 26.5 all-gather.13
  80.2 25.7 all-gather.11
  145.7 130.6 all-reduce.5
  293.7 128.1 all-reduce.7
  486.1 130.6 all-reduce.5
  634.2 128.1 all-reduce.7
  826.7 130.6 all-reduce.5
  974.8 128.1 all-reduce.7
  1186.9 129.2 all-reduce.9
  1357.6 127.2 all-reduce.11
  1549.1 127.3 all-reduce.9
  1717.8 127.2 all-reduce.11
  1909.2 127.3 all-reduce.9
  2077.8 127.2 all-reduce.11
  2257.6 18.3 reduce-scatter.26
  2278.9 20.2 reduce-scatter.28
  2302.2 23.7 reduce-scatter.20
  2328.6 30.9 reduce-scatter.18
  2362.0 34.7 reduce-scatter.22
  2399.3 34.7 reduce-scatter.24
where the time goes:
time: 2450 us; the launch traced here: 2440 us
  waiting for transfers between devices  1730 us (71%)
  matrix products  218 us (9%)
  other arithmetic  196 us (8%)
  local copies, waits for them, and re-layouts  184 us (8%)
  blocking collectives  46.4 us (2%)
  loops' own time  41.8 us (2%)
    psum x3, waiting for transfers between devices, layer_forward(): hidden = token_rows + lax.psum(attn_term, 'tensor') + shift_rows[1]  392 us
    psum x3, waiting for transfers between devices, layer_forward(): lax.psum(mlp_term, 'tensor')  373 us
    psum x3, waiting for transfers between devices, layer_backward(): grad_normed_two = lax.psum(two_term, 'tensor')  343 us
    psum x3, waiting for transfers between devices, layer_backward(): grad_normed_one = lax.psum(one_term, 'tensor')  315 us
    ppermute x6, waiting for transfers between devices, from_behind(): lax.ppermute(value, axis, [(source, source + steps) for source in range(l...  193 us
    unnamed x15, waiting for transfers between devices  80.8 us
    dynamic_update_slice x27, other arithmetic, per_device(): lax.scan(forward_tick, jnp.zeros_like(images[0]), ticks)[1]  69.8 us
  transfers between devices with their start and end apart: 27, of which 23 were waited for; matrix products, arithmetic and copies ran while one was open for 11% of the time, Pallas kernels for 0%

commit v1 on v0

--- a/solution.py
+++ b/solution.py
@@ -193,7 +193,11 @@
     )
     one_term = jnp.einsum("cte,cde->td", grad_proj, qkv_weight, preferred_element_type=jnp.float32)
     token_rows = layer_input.astype(jnp.float32).reshape(-1, model_width)
-    grad_normed_one = lax.psum(one_term, "tensor")
+    grad_normed_one = one_term
+    for hop in (1, 2):
+        grad_normed_one = grad_normed_one + lax.ppermute(
+            grad_normed_one, "tensor", [(dev, dev ^ hop) for dev in range(4)]
+        )
     centred_one, inverse_one = norm_forward(token_rows, gain_rows[0], shift_rows[0])[1:]
     from_one, gain_one_grad, shift_one_grad = norm_backward(
         grad_normed_one, centred_one, inverse_one, gain_rows[0]

time: 2450 us -> 2740 us (1.12)
  waiting for transfers between devices: 1730 us -> 2010 us
    ppermute x0 -> x6, waiting for transfers between devices: none -> 597 us  [layer_backward(): lax.ppermute(grad_normed_one, 'tensor', [(dev, dev ^ hop) for dev in rang...]
    psum x3 -> x0, waiting for transfers between devices: 315 us -> none  [layer_backward(): grad_normed_one = lax.psum(one_term, 'tensor')]
  transfers between devices with their start and end apart: 27 -> 30, of which waited for: 23 -> 26; matrix products, arithmetic and copies ran while one was open for 11% -> 10% of each run, Pallas kernels for 0% -> 0%
where the time goes in v1:
time: 2740 us; the launch traced here: 2730 us
  waiting for transfers between devices  2010 us (73%)
  matrix products  213 us (8%)
  other arithmetic  204 us (7%)
  local copies, waits for them, and re-layouts  184 us (7%)
  blocking collectives  46.6 us (2%)
  loops' own time  41.7 us (2%)
    ppermute x6, waiting for transfers between devices, layer_backward(): lax.ppermute(grad_normed_one, 'tensor', [(dev, dev ^ hop) for dev in rang...  597 us
    psum x3, waiting for transfers between devices, layer_forward(): hidden = token_rows + lax.psum(attn_term, 'tensor') + shift_rows[1]  392 us
    psum x3, waiting for transfers between devices, layer_forward(): lax.psum(mlp_term, 'tensor')  373 us
    psum x3, waiting for transfers between devices, layer_backward(): grad_normed_two = lax.psum(two_term, 'tensor')  343 us
    ppermute x6, waiting for transfers between devices, from_behind(): lax.ppermute(value, axis, [(source, source + steps) for source in range(l...  194 us
    unnamed x15, waiting for transfers between devices  80.5 us
    dynamic_update_slice x27, other arithmetic, per_device(): lax.scan(forward_tick, jnp.zeros_like(images[0]), ticks)[1]  69.7 us
  transfers between devices with their start and end apart: 30, of which 26 were waited for; matrix products, arithmetic and copies ran while one was open for 10% of the time, Pallas kernels for 0%

profile of v1, /device:TPU:0, one launch (start us, length us, event | category | flops | bytes accessed | tf_op | source)
XLA Modules:
  0.0 2734.5 jit_solution(2380726371527977574)
XLA Ops:
  12.3 19.3 all-gather.3
  35.6 12.4 all-gather
  51.1 8.1 all-gather.1
  65.6 7.1 copy.121
  72.7 5.9 all-gather.14.cloned.1.call-done
  78.7 5.1 copy.122
  83.8 22.2 all-gather.12.cloned.1.call-done
  112.5 1034.4 %while.66 = (s32[]{:T(128)}, bf16[1,729,1152]{2,1,0:T(8,128)(2,1)}, bf16[3,1,729,1152]{3,2,1,0:T(8,128)(2,1)}, bf16[3,1,729,1152]{3,2,1,0:T(8,128)(2,1)}, bf16[3...) while((s32[]{:T(128)}, bf16[1,729,1152]{2,1,0:T(8,128)(2,1)}, ...), condition=%wide.region_9.10_spmd, body=%wide.region_0.9_spmd.sunk | while | flops 6232035840 | bytes 263704656 | solution.py:251
  145.6 130.7 %all-reduce.5.cloned.1.call-done = f32[729,1152]{1,0:T(8,128)} async-done(((f32[729,1152]{1,0:T(8,128)}), f32[729,1152]{1,0:T(8,128)}) %all-reduce.5.cloned.1.call-update) | async-done | bytes 3359248 | tf_op jit(solution)/shard_map/while/body/eval_jaxpr/psum | solution.py:86
  297.6 124.3 %all-reduce.7.cloned.1.call-done = f32[729,1152]{1,0:T(8,128)} async-done(((f32[729,1152]{1,0:T(8,128)}), f32[729,1152]{1,0:T(8,128)}) %all-reduce.7.cloned.1.call-update) | async-done | bytes 3359248 | tf_op jit(solution)/shard_map/while/body/eval_jaxpr/psum | solution.py:93
  436.2 29.8 %collective-permute-done = bf16[1,729,1152]{2,1,0:T(8,128)(2,1)} collective-permute-done((bf16[1,729,1152]{2,1,0:T(8,128)(2,1)}, bf16[1,729,1152]{2,1,0:T(8,128)(2,1)}, u32[]{:S(2)}, u32[]{:S(2)}) %collective-permute-start) | collective-permute-done | bytes 1679648 | tf_op jit(solution)/shard_map/while/body/eval_jaxpr/ppermute | solution.py:15
  486.1 130.7 %all-reduce.5.cloned.1.call-done = f32[729,1152]{1,0:T(8,128)} async-done(((f32[729,1152]{1,0:T(8,128)}), f32[729,1152]{1,0:T(8,128)}) %all-reduce.5.cloned.1.call-update) | async-done | bytes 3359248 | tf_op jit(solution)/shard_map/while/body/eval_jaxpr/psum | solution.py:86
  616.8 4.7 bitcast_dynamic-update-slice_fusion.17
  638.0 124.3 %all-reduce.7.cloned.1.call-done = f32[729,1152]{1,0:T(8,128)} async-done(((f32[729,1152]{1,0:T(8,128)}), f32[729,1152]{1,0:T(8,128)}) %all-reduce.7.cloned.1.call-update) | async-done | bytes 3359248 | tf_op jit(solution)/shard_map/while/body/eval_jaxpr/psum | solution.py:93
  776.7 29.7 %collective-permute-done = bf16[1,729,1152]{2,1,0:T(8,128)(2,1)} collective-permute-done((bf16[1,729,1152]{2,1,0:T(8,128)(2,1)}, bf16[1,729,1152]{2,1,0:T(8,128)(2,1)}, u32[]{:S(2)}, u32[]{:S(2)}) %collective-permute-start) | collective-permute-done | bytes 1679648 | tf_op jit(solution)/shard_map/while/body/eval_jaxpr/ppermute | solution.py:15
  826.6 130.8 %all-reduce.5.cloned.1.call-done = f32[729,1152]{1,0:T(8,128)} async-done(((f32[729,1152]{1,0:T(8,128)}), f32[729,1152]{1,0:T(8,128)}) %all-reduce.5.cloned.1.call-update) | async-done | bytes 3359248 | tf_op jit(solution)/shard_map/while/body/eval_jaxpr/psum | solution.py:86
  957.3 4.7 bitcast_dynamic-update-slice_fusion.17
  978.6 124.3 %all-reduce.7.cloned.1.call-done = f32[729,1152]{1,0:T(8,128)} async-done(((f32[729,1152]{1,0:T(8,128)}), f32[729,1152]{1,0:T(8,128)}) %all-reduce.7.cloned.1.call-update) | async-done | bytes 3359248 | tf_op jit(solution)/shard_map/while/body/eval_jaxpr/psum | solution.py:93
  1117.1 29.8 %collective-permute-done = bf16[1,729,1152]{2,1,0:T(8,128)(2,1)} collective-permute-done((bf16[1,729,1152]{2,1,0:T(8,128)(2,1)}, bf16[1,729,1152]{2,1,0:T(8,128)(2,1)}, u32[]{:S(2)}, u32[]{:S(2)}) %collective-permute-start) | collective-permute-done | bytes 1679648 | tf_op jit(solution)/shard_map/while/body/eval_jaxpr/ppermute | solution.py:15
  1149.8 1394.6 %while.67 = (s32[]{:T(128)}, f32[729,1152]{1,0:T(8,128)S(1)}, f32[3,1152,288]{1,2,0:T(8,128)}, f32[288,1152]{1,0:T(8,128)}, f32[1152,1076]{0,1:T(8,128)}, /*inde...) while((s32[]{:T(128)}, f32[729,1152]{1,0:T(8,128)S(1)}, ...), condition=%wide.region_30.31_spmd.clone, body=%wide.region_10.30_spmd.clone.sunk | while | flops 12739572736 | bytes 500847136 | solution.py:283
  1175.0 6.1 convert_reduce_fusion.16
  1195.6 4.9 fusion.211
  1200.5 115.7 %all-reduce.9.cloned.1.call-done = f32[729,1152]{1,0:T(8,128)} async-done(((f32[729,1152]{1,0:T(8,128)}), f32[729,1152]{1,0:T(8,128)}) %all-reduce.9.cloned.1.call-update) | async-done | bytes 3359248 | tf_op jit(solution)/shard_map/while/body/eval_jaxpr/psum | solution.py:138
  1327.0 4.7 multiply_reduce_fusion.17
  1331.6 10.2 multiply_convert_fusion.2
  1347.2 5.5 convert_reduce_fusion.19
  1355.7 74.9 %collective-permute-done.1 = f32[729,1152]{1,0:T(8,128)S(1)} collective-permute-done((f32[729,1152]{1,0:T(8,128)S(1)}, f32[729,1152]{1,0:T(8,128)S(1)}, u32[]{:S(2)}, u32[]{:S(2)}) %collective-permute-start.1) | collective-permute-done | bytes 3359264 | tf_op jit(solution)/shard_map/while/body/eval_jaxpr/ppermute | solution.py:198
  1438.6 6.2 fusion.215
  1444.9 5.2 fusion.216
  1455.4 125.5 %collective-permute-done.2 = f32[729,1152]{1,0:T(8,128)} collective-permute-done((f32[729,1152]{1,0:T(8,128)}, f32[729,1152]{1,0:T(8,128)}, u32[]{:S(2)}, u32[]{:S(2)}) %collective-permute-start.2) | collective-permute-done | bytes 3359264 | tf_op jit(solution)/shard_map/while/body/eval_jaxpr/ppermute | solution.py:198
  1580.9 4.7 fusion.213
  1595.1 35.0 %collective-permute-done.3 = bf16[1,729,1152]{2,1,0:T(8,128)(2,1)S(1)} collective-permute-done((bf16[1,729,1152]{2,1,0:T(8,128)(2,1)S(1)}, bf16[1,729,1152]{2,1,0:T(8,128)(2,1)S(1)}, u32[]{:S(2)}, u32[]{:S(2)}) %collective-permute-start.3) | collective-permute-done | bytes 1679648 | tf_op jit(solution)/shard_map/while/body/eval_jaxpr/ppermute | solution.py:15
  1634.0 6.1 convert_reduce_fusion.16
  1654.7 4.9 fusion.211
  1659.6 113.5 %all-reduce.9.cloned.1.call-done = f32[729,1152]{1,0:T(8,128)} async-done(((f32[729,1152]{1,0:T(8,128)}), f32[729,1152]{1,0:T(8,128)}) %all-reduce.9.cloned.1.call-update) | async-done | bytes 3359248 | tf_op jit(solution)/shard_map/while/body/eval_jaxpr/psum | solution.py:138
  1783.9 4.7 multiply_reduce_fusion.17
  1788.5 10.2 multiply_convert_fusion.2
  1804.1 5.5 convert_reduce_fusion.19
  1812.6 74.9 %collective-permute-done.1 = f32[729,1152]{1,0:T(8,128)S(1)} collective-permute-done((f32[729,1152]{1,0:T(8,128)S(1)}, f32[729,1152]{1,0:T(8,128)S(1)}, u32[]{:S(2)}, u32[]{:S(2)}) %collective-permute-start.1) | collective-permute-done | bytes 3359264 | tf_op jit(solution)/shard_map/while/body/eval_jaxpr/ppermute | solution.py:198
  1895.5 7.7 fusion.215
  1903.3 5.2 fusion.216
  1914.3 123.5 %collective-permute-done.2 = f32[729,1152]{1,0:T(8,128)} collective-permute-done((f32[729,1152]{1,0:T(8,128)}, f32[729,1152]{1,0:T(8,128)}, u32[]{:S(2)}, u32[]{:S(2)}) %collective-permute-start.2) | collective-permute-done | bytes 3359264 | tf_op jit(solution)/shard_map/while/body/eval_jaxpr/ppermute | solution.py:198
  2037.8 4.7 fusion.213
  2051.9 35.0 %collective-permute-done.3 = bf16[1,729,1152]{2,1,0:T(8,128)(2,1)S(1)} collective-permute-done((bf16[1,729,1152]{2,1,0:T(8,128)(2,1)S(1)}, bf16[1,729,1152]{2,1,0:T(8,128)(2,1)S(1)}, u32[]{:S(2)}, u32[]{:S(2)}) %collective-permute-start.3) | collective-permute-done | bytes 1679648 | tf_op jit(solution)/shard_map/while/body/eval_jaxpr/ppermute | solution.py:15
  2090.9 6.1 convert_reduce_fusion.16
  2111.6 4.9 fusion.211
  2116.4 113.5 %all-reduce.9.cloned.1.call-done = f32[729,1152]{1,0:T(8,128)} async-done(((f32[729,1152]{1,0:T(8,128)}), f32[729,1152]{1,0:T(8,128)}) %all-reduce.9.cloned.1.call-update) | async-done | bytes 3359248 | tf_op jit(solution)/shard_map/while/body/eval_jaxpr/psum | solution.py:138
  2240.6 4.7 multiply_reduce_fusion.17
  2245.2 10.2 multiply_convert_fusion.2
  2260.8 5.5 convert_reduce_fusion.19
  2269.3 74.9 %collective-permute-done.1 = f32[729,1152]{1,0:T(8,128)S(1)} collective-permute-done((f32[729,1152]{1,0:T(8,128)S(1)}, f32[729,1152]{1,0:T(8,128)S(1)}, u32[]{:S(2)}, u32[]{:S(2)}) %collective-permute-start.1) | collective-permute-done | bytes 3359264 | tf_op jit(solution)/shard_map/while/body/eval_jaxpr/ppermute | solution.py:198
  2352.2 7.7 fusion.215
  2359.9 5.2 fusion.216
  2370.9 123.5 %collective-permute-done.2 = f32[729,1152]{1,0:T(8,128)} collective-permute-done((f32[729,1152]{1,0:T(8,128)}, f32[729,1152]{1,0:T(8,128)}, u32[]{:S(2)}, u32[]{:S(2)}) %collective-permute-start.2) | collective-permute-done | bytes 3359264 | tf_op jit(solution)/shard_map/while/body/eval_jaxpr/ppermute | solution.py:198
  2494.4 4.8 fusion.213
  2508.7 35.0 %collective-permute-done.3 = bf16[1,729,1152]{2,1,0:T(8,128)(2,1)S(1)} collective-permute-done((bf16[1,729,1152]{2,1,0:T(8,128)(2,1)S(1)}, bf16[1,729,1152]{2,1,0:T(8,128)(2,1)S(1)}, u32[]{:S(2)}, u32[]{:S(2)}) %collective-permute-start.3) | collective-permute-done | bytes 1679648 | tf_op jit(solution)/shard_map/while/body/eval_jaxpr/ppermute | solution.py:15
  2552.8 6.0 copy.137
  2575.8 6.0 copy.129
  2581.8 5.2 constant_dynamic-slice_fusion.3
  2587.0 31.6 %rev.4 = bf16[2,1,729,1152]{3,0,2,1:T(2,128)(2,1)} reverse(bf16[2,1,729,1152]{3,0,2,1:T(2,128)(2,1)} %constant_dynamic-slice_fusion.3), dimensions={0} | reverse | bytes 6718464 | tf_op jit(solution)/shard_map/jit(_flip)/rev | solution.py:307
  2625.2 6.7 all-reduce
  2637.0 13.0 reduce-scatter.19.cloned.1.call-done
  2655.1 32.0 %reduce-scatter.23.cloned.1.call-done = bf16[288,1076]{1,0:T(8,128)(2,1)} async-done(((bf16[1152,1076]{1,0:T(8,128)(2,1)}), bf16[288,1076]{1,0:T(8,128)(2,1)}) %reduce-scatter.23.cloned.1.call-update) | async-done | bytes 619792
  2690.3 34.0 %reduce-scatter.25.cloned.1.call-done = bf16[288,1076]{1,0:T(8,128)(2,1)} async-done(((bf16[1152,1076]{1,0:T(8,128)(2,1)}), bf16[288,1076]{1,0:T(8,128)(2,1)}) %reduce-scatter.25.cloned.1.call-update) | async-done | bytes 619792
  (758 shorter events, 408.8 us)
Async XLA Ops:
  7.2 58.4 %all-gather.10.cloned.1.call-start = ((), (), s32[]{:S(2)}) async-start(), calls=%async_computation.6 | async-start | bytes 4423680 | tf_op jit(solution)/shard_map/all_gather | solution.py:232
  9.8 25.6 copy-start.64
  9.8 68.9 %all-gather.14.cloned.1.call-start = ((), (), s32[]{:S(2)}) async-start(), calls=%async_computation.8 | async-start | bytes 3317760 | tf_op jit(solution)/shard_map/all_gather | solution.py:235
  10.5 95.4 %all-gather.12.cloned.1.call-start = ((), (), s32[]{:S(2)}) async-start(), calls=%async_computation.7 | async-start | bytes 3317760 | tf_op jit(solution)/shard_map/all_gather | solution.py:234
  125.5 150.8 %all-reduce.5.cloned.1.call-start = ((), (), s32[]{:S(2)}) async-start(), calls=%async_computation.15 | async-start | bytes 6782976 | tf_op jit(solution)/shard_map/while/body/eval_jaxpr/psum | solution.py:86
  142.6 133.7 %copy-start.41 = (f32[1152]{0:T(1024)S(1)}, f32[1152]{0:T(1024)}, u32[]{:S(2)}) copy-start(f32[1152]{0:T(1024)} %get-tuple-element.1534) | copy-start | bytes 13828 | tf_op jit(solution)/shard_map/while
  145.6 276.4 %all-reduce.7.cloned.1.call-start = ((), (), s32[]{:S(2)}) async-start(), calls=%async_computation.16 | async-start | bytes 6782976 | tf_op jit(solution)/shard_map/while/body/eval_jaxpr/psum | solution.py:93
  293.6 128.4 %copy-start.42 = (f32[1152]{0:T(1024)S(1)}, f32[1152]{0:T(1024)}, u32[]{:S(2)}) copy-start(f32[1152]{0:T(1024)} %get-tuple-element.1533) | copy-start | bytes 13828 | tf_op jit(solution)/shard_map/while
  422.0 8.8 copy-start.20
  426.1 39.8 %collective-permute-start = (bf16[1,729,1152]{2,1,0:T(8,128)(2,1)}, bf16[1,729,1152]{2,1,0:T(8,128)(2,1)}, u32[]{:S(2)}, u32[]{:S(2)}) collective-permute-start(bf16[1,729,1152]{2,1,0:T(8,128)(2,1)} %bitcast.319), channel_id=1, source_target_pairs={{0,16},{1,17},{2,18},{3,19},{4,20},{5,21},{6,22},{7,23},{8,24},{9,... | collective-permute-start | bytes 5038856 | tf_op jit(solution)/shard_map/while/body/eval_jaxpr/ppermute | solution.py:15
  433.9 32.0 %copy-start.28 = (bf16[2,1,729,1152]{3,2,1,0:T(8,128)(2,1)S(1)}, bf16[2,1,729,1152]{3,2,1,0:T(8,128)(2,1)}, u32[]{:S(2)}) copy-start(bf16[2,1,729,1152]{3,2,1,0:T(8,128)(2,1)} %copy-done.27) | copy-start | bytes 10077700 | tf_op jit(solution)/shard_map/while
  433.9 32.0 %copy-start.45 = (bf16[2,1152]{1,0:T(2,128)(2,1)S(1)}, bf16[2,1152]{1,0:T(2,128)(2,1)}, u32[]{:S(2)}) copy-start(bf16[2,1152]{1,0:T(2,128)(2,1)} %copy-done.44) | copy-start | bytes 13828 | tf_op jit(solution)/shard_map/while
  433.9 32.0 %copy-start.50 = (bf16[4,1152]{1,0:T(4,128)(2,1)S(1)}, bf16[4,1152]{1,0:T(4,128)(2,1)}, u32[]{:S(2)}) copy-start(bf16[4,1152]{1,0:T(4,128)(2,1)} %copy-done.49) | copy-start | bytes 27652 | tf_op jit(solution)/shard_map/while
  433.9 32.0 %copy-start.60 = (bf16[1,2,288]{2,1,0:T(2,128)(2,1)S(1)}, bf16[1,2,288]{2,1,0:T(2,128)(2,1)}, u32[]{:S(2)}) copy-start(bf16[1,2,288]{2,1,0:T(2,128)(2,1)} %get-tuple-element.1900) | copy-start | bytes 3460 | tf_op jit(solution)/shard_map/while
  433.9 32.0 %copy-start.68 = (s32[3]{0:T(128)S(1)}, s32[3]{0:T(128)}, u32[]{:S(2)}) copy-start(s32[3]{0:T(128)} %copy-done.67) | copy-start | bytes 40 | tf_op jit(solution)/shard_map/while
  466.0 150.8 %all-reduce.5.cloned.1.call-start = ((), (), s32[]{:S(2)}) async-start(), calls=%async_computation.15 | async-start | bytes 6782976 | tf_op jit(solution)/shard_map/while/body/eval_jaxpr/psum | solution.py:86
  483.1 133.7 %copy-start.41 = (f32[1152]{0:T(1024)S(1)}, f32[1152]{0:T(1024)}, u32[]{:S(2)}) copy-start(f32[1152]{0:T(1024)} %get-tuple-element.1534) | copy-start | bytes 13828 | tf_op jit(solution)/shard_map/while
  486.0 276.4 %all-reduce.7.cloned.1.call-start = ((), (), s32[]{:S(2)}) async-start(), calls=%async_computation.16 | async-start | bytes 6782976 | tf_op jit(solution)/shard_map/while/body/eval_jaxpr/psum | solution.py:93
  634.0 128.4 %copy-start.42 = (f32[1152]{0:T(1024)S(1)}, f32[1152]{0:T(1024)}, u32[]{:S(2)}) copy-start(f32[1152]{0:T(1024)} %get-tuple-element.1533) | copy-start | bytes 13828 | tf_op jit(solution)/shard_map/while
  762.4 8.8 copy-start.20
  766.6 39.8 %collective-permute-start = (bf16[1,729,1152]{2,1,0:T(8,128)(2,1)}, bf16[1,729,1152]{2,1,0:T(8,128)(2,1)}, u32[]{:S(2)}, u32[]{:S(2)}) collective-permute-start(bf16[1,729,1152]{2,1,0:T(8,128)(2,1)} %bitcast.319), channel_id=1, source_target_pairs={{0,16},{1,17},{2,18},{3,19},{4,20},{5,21},{6,22},{7,23},{8,24},{9,... | collective-permute-start | bytes 5038856 | tf_op jit(solution)/shard_map/while/body/eval_jaxpr/ppermute | solution.py:15
  774.4 32.0 %copy-start.28 = (bf16[2,1,729,1152]{3,2,1,0:T(8,128)(2,1)S(1)}, bf16[2,1,729,1152]{3,2,1,0:T(8,128)(2,1)}, u32[]{:S(2)}) copy-start(bf16[2,1,729,1152]{3,2,1,0:T(8,128)(2,1)} %copy-done.27) | copy-start | bytes 10077700 | tf_op jit(solution)/shard_map/while
  774.4 32.0 %copy-start.45 = (bf16[2,1152]{1,0:T(2,128)(2,1)S(1)}, bf16[2,1152]{1,0:T(2,128)(2,1)}, u32[]{:S(2)}) copy-start(bf16[2,1152]{1,0:T(2,128)(2,1)} %copy-done.44) | copy-start | bytes 13828 | tf_op jit(solution)/shard_map/while
  774.4 32.0 %copy-start.50 = (bf16[4,1152]{1,0:T(4,128)(2,1)S(1)}, bf16[4,1152]{1,0:T(4,128)(2,1)}, u32[]{:S(2)}) copy-start(bf16[4,1152]{1,0:T(4,128)(2,1)} %copy-done.49) | copy-start | bytes 27652 | tf_op jit(solution)/shard_map/while
  774.4 32.0 %copy-start.60 = (bf16[1,2,288]{2,1,0:T(2,128)(2,1)S(1)}, bf16[1,2,288]{2,1,0:T(2,128)(2,1)}, u32[]{:S(2)}) copy-start(bf16[1,2,288]{2,1,0:T(2,128)(2,1)} %get-tuple-element.1900) | copy-start | bytes 3460 | tf_op jit(solution)/shard_map/while
  774.4 32.0 %copy-start.68 = (s32[3]{0:T(128)S(1)}, s32[3]{0:T(128)}, u32[]{:S(2)}) copy-start(s32[3]{0:T(128)} %copy-done.67) | copy-start | bytes 40 | tf_op jit(solution)/shard_map/while
  806.5 150.8 %all-reduce.5.cloned.1.call-start = ((), (), s32[]{:S(2)}) async-start(), calls=%async_computation.15 | async-start | bytes 6782976 | tf_op jit(solution)/shard_map/while/body/eval_jaxpr/psum | solution.py:86
  823.6 133.8 %copy-start.41 = (f32[1152]{0:T(1024)S(1)}, f32[1152]{0:T(1024)}, u32[]{:S(2)}) copy-start(f32[1152]{0:T(1024)} %get-tuple-element.1534) | copy-start | bytes 13828 | tf_op jit(solution)/shard_map/while
  826.5 276.4 %all-reduce.7.cloned.1.call-start = ((), (), s32[]{:S(2)}) async-start(), calls=%async_computation.16 | async-start | bytes 6782976 | tf_op jit(solution)/shard_map/while/body/eval_jaxpr/psum | solution.py:93
  974.6 128.4 %copy-start.42 = (f32[1152]{0:T(1024)S(1)}, f32[1152]{0:T(1024)}, u32[]{:S(2)}) copy-start(f32[1152]{0:T(1024)} %get-tuple-element.1533) | copy-start | bytes 13828 | tf_op jit(solution)/shard_map/while
  1102.9 8.7 copy-start.20
  1107.0 39.8 %collective-permute-start = (bf16[1,729,1152]{2,1,0:T(8,128)(2,1)}, bf16[1,729,1152]{2,1,0:T(8,128)(2,1)}, u32[]{:S(2)}, u32[]{:S(2)}) collective-permute-start(bf16[1,729,1152]{2,1,0:T(8,128)(2,1)} %bitcast.319), channel_id=1, source_target_pairs={{0,16},{1,17},{2,18},{3,19},{4,20},{5,21},{6,22},{7,23},{8,24},{9,... | collective-permute-start | bytes 5038856 | tf_op jit(solution)/shard_map/while/body/eval_jaxpr/ppermute | solution.py:15
  1114.8 32.0 %copy-start.28 = (bf16[2,1,729,1152]{3,2,1,0:T(8,128)(2,1)S(1)}, bf16[2,1,729,1152]{3,2,1,0:T(8,128)(2,1)}, u32[]{:S(2)}) copy-start(bf16[2,1,729,1152]{3,2,1,0:T(8,128)(2,1)} %copy-done.27) | copy-start | bytes 10077700 | tf_op jit(solution)/shard_map/while
  1114.8 32.0 %copy-start.45 = (bf16[2,1152]{1,0:T(2,128)(2,1)S(1)}, bf16[2,1152]{1,0:T(2,128)(2,1)}, u32[]{:S(2)}) copy-start(bf16[2,1152]{1,0:T(2,128)(2,1)} %copy-done.44) | copy-start | bytes 13828 | tf_op jit(solution)/shard_map/while
  1114.8 32.0 %copy-start.50 = (bf16[4,1152]{1,0:T(4,128)(2,1)S(1)}, bf16[4,1152]{1,0:T(4,128)(2,1)}, u32[]{:S(2)}) copy-start(bf16[4,1152]{1,0:T(4,128)(2,1)} %copy-done.49) | copy-start | bytes 27652 | tf_op jit(solution)/shard_map/while
  1114.8 32.0 %copy-start.60 = (bf16[1,2,288]{2,1,0:T(2,128)(2,1)S(1)}, bf16[1,2,288]{2,1,0:T(2,128)(2,1)}, u32[]{:S(2)}) copy-start(bf16[1,2,288]{2,1,0:T(2,128)(2,1)} %get-tuple-element.1900) | copy-start | bytes 3460 | tf_op jit(solution)/shard_map/while
  1114.9 32.0 %copy-start.68 = (s32[3]{0:T(128)S(1)}, s32[3]{0:T(128)}, u32[]{:S(2)}) copy-start(s32[3]{0:T(128)} %copy-done.67) | copy-start | bytes 40 | tf_op jit(solution)/shard_map/while
  1171.3 144.9 %all-reduce.9.cloned.1.call-start = ((), (), s32[]{:S(2)}) async-start(), calls=%async_computation.17 | async-start | bytes 6782976 | tf_op jit(solution)/shard_map/while/body/eval_jaxpr/psum | solution.py:138
  1355.7 75.0 %collective-permute-start.1 = (f32[729,1152]{1,0:T(8,128)S(1)}, f32[729,1152]{1,0:T(8,128)S(1)}, u32[]{:S(2)}, u32[]{:S(2)}) collective-permute-start(f32[729,1152]{1,0:T(8,128)S(1)} %convolution_bitcast_fusion.5), channel_id=1, source_target_pairs={{0,4},{4,0},{8,12},{12,8},{1,5},{5,1},{9,13},{13,9},{2,6},{6,2},{1... | collective-permute-start | bytes 10077704 | tf_op jit(solution)/shard_map/while/body/eval_jaxpr/ppermute | solution.py:198
  1432.9 148.0 %collective-permute-start.2 = (f32[729,1152]{1,0:T(8,128)}, f32[729,1152]{1,0:T(8,128)}, u32[]{:S(2)}, u32[]{:S(2)}) collective-permute-start(f32[729,1152]{1,0:T(8,128)} %add.588), channel_id=1, source_target_pairs={{0,8},{4,12},{8,0},{12,4},{1,9},{5,13},{9,1},{13,5},{2,10},{6,14},... | collective-permute-start | bytes 10077704 | tf_op jit(solution)/shard_map/while/body/eval_jaxpr/ppermute | solution.py:198
  1434.3 10.6 slice-start.3
  1589.3 40.8 %collective-permute-start.3 = (bf16[1,729,1152]{2,1,0:T(8,128)(2,1)S(1)}, bf16[1,729,1152]{2,1,0:T(8,128)(2,1)S(1)}, u32[]{:S(2)}, u32[]{:S(2)}) collective-permute-start(bf16[1,729,1152]{2,1,0:T(8,128)(2,1)S(1)} %bitcast.382), channel_id=1, source_target_pairs={{16,0},{17,1},{18,2},{19,3},{20,4},{21,5},{22,6},{23,7},{24,8},{25... | collective-permute-start | bytes 5038856 | tf_op jit(solution)/shard_map/while/body/eval_jaxpr/ppermute | solution.py:15
  1595.0 35.3 %copy-start.32 = (f32[3,1152,288]{1,2,0:T(8,128)}, f32[3,1152,288]{1,2,0:T(8,128)S(1)}, u32[]{:S(2)}) copy-start(f32[3,1152,288]{1,2,0:T(8,128)S(1)} %bitcast_add_fusion.2) | copy-start | bytes 11943940 | tf_op jit(solution)/shard_map/while
  1630.3 142.8 %all-reduce.9.cloned.1.call-start = ((), (), s32[]{:S(2)}) async-start(), calls=%async_computation.17 | async-start | bytes 6782976 | tf_op jit(solution)/shard_map/while/body/eval_jaxpr/psum | solution.py:138
  1812.6 75.0 %collective-permute-start.1 = (f32[729,1152]{1,0:T(8,128)S(1)}, f32[729,1152]{1,0:T(8,128)S(1)}, u32[]{:S(2)}, u32[]{:S(2)}) collective-permute-start(f32[729,1152]{1,0:T(8,128)S(1)} %convolution_bitcast_fusion.5), channel_id=1, source_target_pairs={{0,4},{4,0},{8,12},{12,8},{1,5},{5,1},{9,13},{13,9},{2,6},{6,2},{1... | collective-permute-start | bytes 10077704 | tf_op jit(solution)/shard_map/while/body/eval_jaxpr/ppermute | solution.py:198
  1889.8 148.0 %collective-permute-start.2 = (f32[729,1152]{1,0:T(8,128)}, f32[729,1152]{1,0:T(8,128)}, u32[]{:S(2)}, u32[]{:S(2)}) collective-permute-start(f32[729,1152]{1,0:T(8,128)} %add.588), channel_id=1, source_target_pairs={{0,8},{4,12},{8,0},{12,4},{1,9},{5,13},{9,1},{13,5},{2,10},{6,14},... | collective-permute-start | bytes 10077704 | tf_op jit(solution)/shard_map/while/body/eval_jaxpr/ppermute | solution.py:198
  1891.2 12.0 slice-start.3
  1895.5 7.7 copy-start.26
  2046.1 40.8 %collective-permute-start.3 = (bf16[1,729,1152]{2,1,0:T(8,128)(2,1)S(1)}, bf16[1,729,1152]{2,1,0:T(8,128)(2,1)S(1)}, u32[]{:S(2)}, u32[]{:S(2)}) collective-permute-start(bf16[1,729,1152]{2,1,0:T(8,128)(2,1)S(1)} %bitcast.382), channel_id=1, source_target_pairs={{16,0},{17,1},{18,2},{19,3},{20,4},{21,5},{22,6},{23,7},{24,8},{25... | collective-permute-start | bytes 5038856 | tf_op jit(solution)/shard_map/while/body/eval_jaxpr/ppermute | solution.py:15
  2051.8 35.3 %copy-start.32 = (f32[3,1152,288]{1,2,0:T(8,128)}, f32[3,1152,288]{1,2,0:T(8,128)S(1)}, u32[]{:S(2)}) copy-start(f32[3,1152,288]{1,2,0:T(8,128)S(1)} %bitcast_add_fusion.2) | copy-start | bytes 11943940 | tf_op jit(solution)/shard_map/while
  2087.2 142.8 %all-reduce.9.cloned.1.call-start = ((), (), s32[]{:S(2)}) async-start(), calls=%async_computation.17 | async-start | bytes 6782976 | tf_op jit(solution)/shard_map/while/body/eval_jaxpr/psum | solution.py:138
  2269.2 75.0 %collective-permute-start.1 = (f32[729,1152]{1,0:T(8,128)S(1)}, f32[729,1152]{1,0:T(8,128)S(1)}, u32[]{:S(2)}, u32[]{:S(2)}) collective-permute-start(f32[729,1152]{1,0:T(8,128)S(1)} %convolution_bitcast_fusion.5), channel_id=1, source_target_pairs={{0,4},{4,0},{8,12},{12,8},{1,5},{5,1},{9,13},{13,9},{2,6},{6,2},{1... | collective-permute-start | bytes 10077704 | tf_op jit(solution)/shard_map/while/body/eval_jaxpr/ppermute | solution.py:198
  2346.5 148.0 %collective-permute-start.2 = (f32[729,1152]{1,0:T(8,128)}, f32[729,1152]{1,0:T(8,128)}, u32[]{:S(2)}, u32[]{:S(2)}) collective-permute-start(f32[729,1152]{1,0:T(8,128)} %add.588), channel_id=1, source_target_pairs={{0,8},{4,12},{8,0},{12,4},{1,9},{5,13},{9,1},{13,5},{2,10},{6,14},... | collective-permute-start | bytes 10077704 | tf_op jit(solution)/shard_map/while/body/eval_jaxpr/ppermute | solution.py:198
  2347.9 12.0 slice-start.3
  2352.2 7.7 copy-start.26
  2352.2 7.7 slice-start.4
  2502.9 40.8 %collective-permute-start.3 = (bf16[1,729,1152]{2,1,0:T(8,128)(2,1)S(1)}, bf16[1,729,1152]{2,1,0:T(8,128)(2,1)S(1)}, u32[]{:S(2)}, u32[]{:S(2)}) collective-permute-start(bf16[1,729,1152]{2,1,0:T(8,128)(2,1)S(1)} %bitcast.382), channel_id=1, source_target_pairs={{16,0},{17,1},{18,2},{19,3},{20,4},{21,5},{22,6},{23,7},{24,8},{25... | collective-permute-start | bytes 5038856 | tf_op jit(solution)/shard_map/while/body/eval_jaxpr/ppermute | solution.py:15
  2508.6 35.3 %copy-start.32 = (f32[3,1152,288]{1,2,0:T(8,128)}, f32[3,1152,288]{1,2,0:T(8,128)S(1)}, u32[]{:S(2)}) copy-start(f32[3,1152,288]{1,2,0:T(8,128)S(1)} %bitcast_add_fusion.2) | copy-start | bytes 11943940 | tf_op jit(solution)/shard_map/while
  2544.4 87.5 %reduce-scatter.27.cloned.1.call-start = ((), (), s32[]{:S(2)}) async-start(), calls=%async_computation.13 | async-start | bytes 368640
  2545.4 88.1 %reduce-scatter.29.cloned.1.call-start = ((), (), s32[]{:S(2)}) async-start(), calls=%async_computation.14 | async-start | bytes 368640
  2546.4 88.6 %reduce-scatter.21.cloned.1.call-start = ((), (), s32[]{:S(2)}) async-start(), calls=%async_computation.10 | async-start | bytes 1105920
  2549.1 100.9 %reduce-scatter.19.cloned.1.call-start = ((), (), s32[]{:S(2)}) async-start(), calls=%async_computation.9 | async-start | bytes 2580480
  2563.0 124.2 %reduce-scatter.23.cloned.1.call-start = ((), (), s32[]{:S(2)}) async-start(), calls=%async_computation.11 | async-start | bytes 3317760
  2569.0 155.3 %reduce-scatter.25.cloned.1.call-start = ((), (), s32[]{:S(2)}) async-start(), calls=%async_computation.12 | async-start | bytes 3317760
  (170 other events, 576.9 us)
Sparse Core Ops, SparseCore 0:
  10.1 40.3 all-gather.9
  52.1 26.5 all-gather.13
  80.2 25.7 all-gather.11
  145.7 130.6 all-reduce.4
  293.7 128.1 all-reduce.6
  486.1 130.6 all-reduce.4
  634.2 128.1 all-reduce.6
  826.6 130.6 all-reduce.4
  974.7 128.1 all-reduce.6
  1186.9 129.2 all-reduce.8
  1645.9 127.1 all-reduce.8
  2102.8 127.1 all-reduce.8
  2548.3 18.1 reduce-scatter.26
  2569.4 20.2 reduce-scatter.28
  2592.7 23.8 reduce-scatter.20
  2619.0 30.9 reduce-scatter.18
  2652.4 34.6 reduce-scatter.22
  2689.5 34.7 reduce-scatter.24
